TPU v7x, 32 devices: a whole 2x2x4 slice. The times are simulated.
32 devices in a mesh: expert: 16 (over z, x, core), dp: 2 (over y).
Axes of the slice: x: 2, y: 2, z: 4, core: 2. Of those that a mesh axis runs over, the one named last changes fastest.
Arguments:
- tokens: bfloat16 [1536, 2880], P(('expert', 'dp')), may hold values from -6 to 6
- expert_ids: int32 [1536, 4], P(('expert', 'dp')), may hold values from 0 to 15, all different within a row; in each aligned block of 48 rows (0 to 47, 48 to 95, ...) at most 24 rows name the same one
- combine_int: int32 [1536, 4], P(('expert', 'dp')), may hold values from 8 to 63
- gate_weight: bfloat16 [16, 2880, 2880], P('expert', None, 'dp'), may hold values from -0.109375 to 0.109375
- up_weight: bfloat16 [16, 2880, 2880], P('expert', None, 'dp'), may hold values from -0.109375 to 0.109375
- down_weight: bfloat16 [16, 2880, 2880], P('expert', 'dp'), may hold values from -0.109375 to 0.109375
Outputs:
- mixed: bfloat16 [1536, 2880], P(('expert', 'dp'))
Inputs may be any that keep to these rules, and one draw needn't show every extreme that they name: `expert_ids`: each row names 4 different experts; within the 48 rows of one device no expert is named by more than 24 rows, a bound that some block reaches.
All inputs are finite; a program needn't handle non-finite values.
Results may differ from a plain program's by a relative error of at most 0.0049.
Values may be sent and summed in bfloat16 or wider, within the bound.
A program may use at most 128 MiB of HBM per device.

v0:
```python
import jax
import jax.numpy as jnp
from jax import lax
from jax.sharding import PartitionSpec as P


def expert_rows(rows, gate_w, up_w, down_w):
    gate = jnp.dot(rows, gate_w, preferred_element_type=jnp.float32)
    up = jnp.dot(rows, up_w, preferred_element_type=jnp.float32)
    hidden = (gate * jax.nn.sigmoid(1.702 * gate) * (up + 1.0)).astype(jnp.bfloat16)
    return jnp.dot(hidden, down_w, preferred_element_type=jnp.float32)


def build_tables(tokens, expert_ids, combine_int, experts, capacity):
    tok_rows, top = expert_ids.shape
    flat_ids = expert_ids.reshape(-1)
    onehot = (flat_ids[:, None] == jnp.arange(experts, dtype=jnp.int32)[None, :]).astype(jnp.int32)
    ranks = jnp.sum(onehot * (jnp.cumsum(onehot, axis=0) - 1), axis=1)
    places = (flat_ids * capacity + ranks).reshape(tok_rows, top)
    slot_ids = jnp.arange(experts * capacity, dtype=jnp.int32)
    matches = places[:, :, None] == slot_ids[None, None, :]
    sender = jnp.any(matches, axis=1).astype(jnp.bfloat16)
    buffer = jnp.dot(sender.T, tokens, preferred_element_type=jnp.float32).astype(jnp.bfloat16)
    weights = combine_int.astype(jnp.float32) / 32.0
    mixing = jnp.sum(jnp.where(matches, weights[:, :, None], 0.0), axis=1)
    return (buffer.reshape(experts, capacity, tokens.shape[1]), mixing)


def shards(tokens, expert_ids, combine_int, gate_weight, up_weight, down_weight):
    experts = lax.axis_size("expert")
    width = tokens.shape[1]
    capacity = 2 * expert_ids.shape[1] * tokens.shape[0] // experts
    gate_w, up_w, down_w = (gate_weight[0], up_weight[0], down_weight[0])
    buffer, mixing = build_tables(tokens, expert_ids, combine_int, experts, capacity)
    received = lax.all_to_all(buffer, "expert", split_axis=0, concat_axis=0, tiled=True)
    piece = lax.all_gather(received, "dp", axis=0, tiled=True)
    result = expert_rows(piece.reshape(-1, width), gate_w, up_w, down_w)
    partials = result.reshape(piece.shape[0], piece.shape[1], width)
    summed = lax.psum_scatter(partials, "dp", scatter_dimension=0, tiled=True)
    back = lax.all_to_all(summed, "expert", split_axis=0, concat_axis=0, tiled=True)
    mixed = jnp.dot(mixing, back.reshape(-1, width), precision=lax.Precision.HIGHEST)
    return mixed.astype(jnp.bfloat16)


def solution(mesh):
    return jax.shard_map(
        shards,
        mesh=mesh,
        in_specs=(
            P(("expert", "dp"), None),
            P(("expert", "dp"), None),
            P(("expert", "dp"), None),
            P("expert", None, "dp"),
            P("expert", None, "dp"),
            P("expert", "dp", None),
        ),
        out_specs=P(("expert", "dp"), None),
        check_vma=False,
    )
```

profile of v0, /device:TPU:11, one launch (start us, length us, event | category | flops | bytes accessed | tf_op | source)
XLA Modules:
  0.0 390.0 jit_solution(13816666832741851455)
XLA Ops:
  6.5 0.0 copy-start
  6.5 0.0 all-gather.2.cloned.1.call-start
  6.5 0.8 copy.34
  7.4 0.1 eq.35
  7.5 0.6 reduce-window.6
  8.1 0.2 slice_reduce_fusion
  8.3 0.1 bitcast_bitcast_fusion
  8.4 0.1 reduce_sum.21
  8.5 0.1 copy.37
  8.6 0.7 multiply_add_fusion
  9.3 0.1 fusion.8
  9.4 0.0 copy-done
  9.4 0.8 convolution_convert_fusion
  10.2 2.6 copy.38
  12.8 57.4 %all_to_all.10 = bf16[16,24,2880]{2,1,0:T(8,128)(2,1)} all-to-all(bf16[16,24,2880]{2,1,0:T(8,128)(2,1)} %bitcast.35), channel_id=1, replica_groups=mesh['expert'=16,'dp'=2] {'expert'}, dimensions={0} | all-to-all | bytes 4423680 | tf_op jit(solution)/shard_map/all_to_all | solution.py:35
  70.2 0.0 all-gather.2.cloned.1.call-update
  70.2 0.0 reduce-scatter.2.cloned.1.call-start
  70.3 60.1 %all-gather.2.cloned.1.call-done = bf16[32,24,2880]{2,1,0:T(8,128)(2,1)} async-done(((bf16[16,24,2880]{2,1,0:T(8,128)(2,1)}), bf16[32,24,2880]{2,1,0:T(8,128)(2,1)}) %all-gather.2.cloned.1.call-update) | async-done | bytes 4423696 | tf_op jit(solution)/shard_map/all_gather | solution.py:36
  130.4 11.0 %fusion.2 = f32[768,1440]{0,1:T(8,128)S(1)} fusion(bf16[768,2880]{1,0:T(8,128)(2,1)} %bitcast.39, bf16[1,2880,1440]{1,2,0:T(8,128)(2,1)} %param.10), kind=kOutput, calls=%fused_computation.2 | convolution fusion | flops 6370099200 | bytes 17141760 | tf_op jit(solution)/shard_map/dot_general | solution.py:9
  141.4 0.0 slice-done
  141.4 0.0 slice-done.1
  141.4 0.0 slice-done.2
  141.4 8.9 %multiply_convert_fusion = bf16[768,1440]{0,1:T(8,128)(2,1)} fusion(f32[768,1440]{0,1:T(8,128)S(1)} %fusion.2, bf16[768,2880]{1,0:T(8,128)(2,1)S(1)} %bitcast.40, bf16[1,2880,1440]{1,2,0:T(8,128)(2,1)S(1)} %bitcast.38), kind=kOutput, calls=%fused_computation.6 | convolution fusion | flops 6378946560 | bytes 19353600 | tf_op jit(solution)/shard_map/dot_general | solution.py:8
  150.3 2.8 copy.39
  153.1 12.1 %fusion = f32[32,24,2880]{2,1,0:T(8,128)} fusion(bf16[32,24,1440]{2,1,0:T(8,128)(2,1)S(1)} %bitcast.36, bf16[1,1440,2880]{2,1,0:T(8,128)(2,1)} %param.11), kind=kOutput, calls=%fused_computation | convolution fusion | flops 6370099200 | bytes 19353600 | tf_op jit(solution)/shard_map/dot_general | solution.py:11
  165.1 0.0 reduce-scatter.2.cloned.1.call-update
  165.2 0.0 copy-start.1
  165.2 106.5 %reduce-scatter.2.cloned.1.call-done = f32[16,24,2880]{2,1,0:T(8,128)} async-done(((f32[32,24,2880]{2,1,0:T(8,128)}), f32[16,24,2880]{2,1,0:T(8,128)}) %reduce-scatter.2.cloned.1.call-update) | async-done | bytes 4423696 | tf_op jit(solution)/shard_map/reduce_scatter | solution.py:39
  271.7 6.5 %all-to-all-start.1 = ((f32[16,24,2880]{2,1,0:T(8,128)}), f32[16,24,2880]{2,1,0:T(8,128)}, u32[]{:S(2)}, u32[]{:S(2)}) async-start(f32[16,24,2880]{2,1,0:T(8,128)} %reduce-scatter.2.cloned.1.call-done), calls=%async_computation.2 | async-start | bytes 9043968 | tf_op jit(solution)/shard_map/all_to_all | solution.py:40
  278.2 0.1 select_reduce_fusion
  278.4 99.3 %all-to-all-done.1 = f32[16,24,2880]{2,1,0:T(8,128)} async-done(((f32[16,24,2880]{2,1,0:T(8,128)}), f32[16,24,2880]{2,1,0:T(8,128)}, u32[]{:S(2)}, u32[]{:S(2)}) %all-to-all-start.1) | async-done | bytes 4423712 | tf_op jit(solution)/shard_map/all_to_all | solution.py:40
  377.7 5.4 %convolution_convert_fusion.1 = bf16[48,2880]{1,0:T(8,128)(2,1)} fusion(f32[48,384]{1,0:T(8,128)S(1)} %select_reduce_fusion, f32[384,2880]{1,0:T(8,128)} %bitcast.8), kind=kOutput, calls=%fused_computation.8 | convolution fusion | flops 637148160 | bytes 4773888 | tf_op jit(solution)/shard_map/dot_general | solution.py:41
  (13 shorter events, 0.1 us)
Async XLA Ops:
  6.5 2.9 copy-start
  6.5 123.9 %all-gather.2.cloned.1.call-start = ((), (), s32[]{:S(2)}) async-start(), calls=%async_computation.3 | async-start | bytes 6782976 | tf_op jit(solution)/shard_map/all_gather | solution.py:36
  70.2 71.2 %slice-start = ((s8[8478720]{0:T(1024)(128)(4,1)}), s8[90112]{0:T(1024)(128)(4,1)S(1)}, s32[]{:S(2)}) async-start(s8[8478720]{0:T(1024)(128)(4,1)} %bitcast.37), calls=%async_computation.5 | async-start | bytes 180224
  70.2 201.5 %reduce-scatter.2.cloned.1.call-start = ((), (), s32[]{:S(2)}) async-start(), calls=%async_computation.4 | async-start | bytes 13565952 | tf_op jit(solution)/shard_map/reduce_scatter | solution.py:39
  130.4 11.0 %slice-start.1 = ((s8[8478720]{0:T(1024)(128)(4,1)}), s8[4194304]{0:T(1024)(128)(4,1)S(1)}, s32[]{:S(2)}) async-start(s8[8478720]{0:T(1024)(128)(4,1)} %bitcast.37), calls=%async_computation.6 | async-start | bytes 8388608
  130.4 11.0 %slice-start.2 = ((s8[8478720]{0:T(1024)(128)(4,1)}), s8[4194304]{0:T(1024)(128)(4,1)S(1)}, s32[]{:S(2)}) async-start(s8[8478720]{0:T(1024)(128)(4,1)} %bitcast.37), calls=%async_computation.7 | async-start | bytes 8388608
  130.4 11.0 %copy-start.2 = (bf16[32,24,2880]{2,1,0:T(8,128)(2,1)S(1)}, bf16[32,24,2880]{2,1,0:T(8,128)(2,1)}, u32[]{:S(2)}) copy-start(bf16[32,24,2880]{2,1,0:T(8,128)(2,1)} %all-gather.2.cloned.1.call-done) | copy-start | bytes 13271044
  165.2 113.1 %copy-start.1 = (s32[48,4]{0,1:T(4,128)S(1)}, s32[48,4]{0,1:T(4,128)}, u32[]{:S(2)}) copy-start(s32[48,4]{0,1:T(4,128)} %param.8) | copy-start | bytes 2308
  271.7 106.0 %all-to-all-start.1 = ((f32[16,24,2880]{2,1,0:T(8,128)}), f32[16,24,2880]{2,1,0:T(8,128)}, u32[]{:S(2)}, u32[]{:S(2)}) async-start(f32[16,24,2880]{2,1,0:T(8,128)} %reduce-scatter.2.cloned.1.call-done), calls=%async_computation.2 | async-start | bytes 9043968 | tf_op jit(solution)/shard_map/all_to_all | solution.py:40
Sparse Core Ops, SparseCore 0:
  70.3 60.0 all-gather.1
  165.3 106.3 reduce-scatter.1
where the time goes:
time: 390 us
  waiting for transfers between devices  266 us (68%)
  blocking collectives  57.4 us (15%)
  matrix products  38.1 us (10%)
  between operations  13.5 us (3%)
  local copies, waits for them, and re-layouts  6.67 us (2%)
  starting transfers between devices  6.55 us (2%)
    reduce_scatter x1, waiting for transfers between devices, shards(): summed = lax.psum_scatter(partials, 'dp', scatter_dimension=0, tiled=True)  107 us
    all_to_all x1, waiting for transfers between devices, shards(): lax.all_to_all(summed, 'expert', split_axis=0, concat_axis=0, tiled=True)  99.3 us
    all_gather x1, waiting for transfers between devices, shards(): piece = lax.all_gather(received, 'dp', axis=0, tiled=True)  60.1 us
    all_to_all x1, blocking collectives, shards(): lax.all_to_all(buffer, 'expert', split_axis=0, concat_axis=0, tiled=True)  57.4 us
    dot_general x1, matrix products, expert_rows(): return jnp.dot(hidden, down_w, preferred_element_type=jnp.float32)  12.1 us
    dot_general x1, matrix products, expert_rows(): up = jnp.dot(rows, up_w, preferred_element_type=jnp.float32)  11 us
    dot_general x1, matrix products, expert_rows(): gate = jnp.dot(rows, gate_w, preferred_element_type=jnp.float32)  8.86 us
  transfers between devices with their start and end apart: 3, of which 3 were waited for; matrix products, arithmetic and copies ran while one was open for 0% of the time, Pallas kernels for 0%

commit v1 on v0

--- a/solution.py
+++ b/solution.py
@@ -1,7 +1,15 @@
+import functools
+
 import jax
 import jax.numpy as jnp
 from jax import lax
+from jax.experimental import pallas as pl
+from jax.experimental.pallas import tpu as pltpu
 from jax.sharding import PartitionSpec as P
+
+MESH = pl.DeviceIdType.MESH
+BF16 = jnp.bfloat16
+F32 = jnp.float32
 
 
 def expert_rows(rows, gate_w, up_w, down_w):
@@ -26,7 +34,7 @@
     return (buffer.reshape(experts, capacity, tokens.shape[1]), mixing)
 
 
-def shards(tokens, expert_ids, combine_int, gate_weight, up_weight, down_weight):
+def padded_plan(tokens, expert_ids, combine_int, gate_weight, up_weight, down_weight):
     experts = lax.axis_size("expert")
     width = tokens.shape[1]
     capacity = 2 * expert_ids.shape[1] * tokens.shape[0] // experts
@@ -40,6 +48,313 @@
     back = lax.all_to_all(summed, "expert", split_axis=0, concat_axis=0, tiled=True)
     mixed = jnp.dot(mixing, back.reshape(-1, width), precision=lax.Precision.HIGHEST)
     return mixed.astype(jnp.bfloat16)
+
+
+def tiles_of(total, step):
+    return total // step, total % step
+
+
+def kernel(experts, cap, tokens, ids, comb, gate_hbm, up_hbm, down_hbm, out,
+           tok, contrib, from_core, from_b, from_a, from_z, picked, hid, gate_w, up_w, down_w,
+           w_sem, send_sem, recv_sem, pair_send, pair_recv, ret_send, b_recv, a_recv, z_recv):
+    rows, width = tokens.shape
+    half = gate_w.shape[1]
+    padded = tok.shape[2]
+    top = ids.shape[1]
+    groups = experts // 4
+    span = 2 * groups
+    me, dp = lax.axis_index("expert"), lax.axis_index("dp")
+    core, side, g = me % 2, (me // 2) % 2, me // 4
+    partner = (me + 1 - 2 * core, dp)
+    a_peer = (me + (1 - core) * (2 - 4 * side), dp + core * (1 - 2 * dp))
+    b_peer = (me + core * (2 - 4 * side), dp + (1 - core) * (1 - 2 * dp))
+
+    def z_peer(j):
+        return (((g + j) % groups) * 4 + me % 4, dp)
+
+    loads = [
+        pltpu.make_async_copy(gate_hbm.at[0], gate_w, w_sem.at[0]),
+        pltpu.make_async_copy(up_hbm.at[0], up_w, w_sem.at[1]),
+        pltpu.make_async_copy(down_hbm.at[0], down_w, w_sem.at[2]),
+    ]
+
+    edge = padded - 128
+    own = width - edge
+    lane = lax.broadcasted_iota(jnp.int32, (rows, 128), 1)
+    hits = jnp.zeros((rows, 128), F32)
+    weights = jnp.zeros((rows, 128), F32)
+    for k in range(top):
+        hits += jnp.where(lane == ids[:, k:k + 1] + own, 1.0, 0.0)
+        weights += jnp.where(lane == ids[:, k:k + 1] + (own + experts), comb[:, k:k + 1].astype(F32), 0.0)
+    below = (lax.broadcasted_iota(jnp.int32, (rows, rows), 0)
+             >= lax.broadcasted_iota(jnp.int32, (rows, rows), 1)).astype(BF16)
+    counts = jnp.dot(below, hits.astype(BF16), preferred_element_type=F32)
+    info = (hits * counts + weights).astype(BF16)
+    tok[0, :, :edge] = tokens[:, :edge]
+    tok[0, :, edge:] = jnp.concatenate([tokens[:, edge:width], info[:, own:]], axis=1)
+
+    barrier = pltpu.get_barrier_semaphore()
+    peers = [partner, a_peer, b_peer] + [z_peer(j) for j in range(1, groups)]
+    for peer in peers:
+        pl.semaphore_signal(barrier, inc=1, device_id=peer, device_id_type=MESH)
+    pl.semaphore_wait(barrier, len(peers))
+
+    def place(k):
+        return (k // groups) * span + k % groups
+
+    def sent(src, dst, sem, peer):
+        return pltpu.make_async_remote_copy(
+            src_ref=tok.at[src], dst_ref=tok.at[dst], send_sem=send_sem.at[sem],
+            recv_sem=recv_sem.at[dst], device_id=peer, device_id_type=MESH)
+
+    def to_z(j):
+        return sent(0, groups - j, j, z_peer(j))
+
+    def to_a(j):
+        return sent(place(j), place(groups + j), groups + j, a_peer)
+
+    def to_b(k):
+        return sent(place(k), place(2 * groups + k), 2 * groups + k, b_peer)
+
+    def to_core(k):
+        return sent(place(k), place(k) + groups, 4 * groups + k, partner)
+
+    def arrived(slot):
+        sent(0, slot, 0, partner).wait_recv()
+
+    for j in range(1, groups):
+        to_z(j).start()
+    to_a(0).start()
+    to_b(0).start()
+    to_core(0).start()
+    for load in loads:
+        load.start()
+    for j in range(1, groups):
+        arrived(place(j))
+        to_a(j).start()
+        to_b(j).start()
+        to_core(j).start()
+    for j in range(groups):
+        arrived(place(groups + j))
+        to_b(groups + j).start()
+        to_core(groups + j).start()
+    for load in loads:
+        load.wait()
+
+    def pair_copy(c):
+        return pltpu.make_async_remote_copy(
+            src_ref=contrib.at[pl.ds(c * span + groups, groups)], dst_ref=from_core.at[pl.ds(c * groups, groups)],
+            send_sem=pair_send.at[c], recv_sem=pair_recv.at[c], device_id=partner, device_id_type=MESH)
+
+    def b_copy(k):
+        return pltpu.make_async_remote_copy(
+            src_ref=contrib.at[place(2 * groups + k)], dst_ref=from_b.at[k],
+            send_sem=ret_send.at[2 * groups + k], recv_sem=b_recv.at[k], device_id=b_peer, device_id_type=MESH)
+
+    def a_copy(j):
+        return pltpu.make_async_remote_copy(
+            src_ref=contrib.at[place(groups + j)], dst_ref=from_a.at[j],
+            send_sem=ret_send.at[groups + j], recv_sem=a_recv.at[j], device_id=a_peer, device_id_type=MESH)
+
+    def z_copy(j):
+        return pltpu.make_async_remote_copy(
+            src_ref=contrib.at[j], dst_ref=from_z.at[groups - j],
+            send_sem=ret_send.at[j], recv_sem=z_recv.at[groups - j], device_id=z_peer(j), device_id_type=MESH)
+
+    def back_to_b(c):
+        pair_copy(c).wait_recv()
+
+        def one(q, _):
+            k = c * groups + q
+            s = place(k)
+            contrib[s] = (contrib[s].astype(F32) + from_core[k].astype(F32)).astype(BF16)
+            b_copy(k - 2 * groups).start()
+            return 0
+
+        lax.fori_loop(0, groups, one, 0)
+
+    chunk_rows = span * cap
+    chunk_toks = span * rows
+
+    def chunk(c):
+        block = tok.at[pl.ds(c * span, span)]
+        tail = block[:, :, edge:].reshape(chunk_toks, 128).astype(F32)
+        tail_lane = lax.broadcasted_iota(jnp.int32, (chunk_toks, 128), 1)
+        rank1 = jnp.sum(jnp.where(tail_lane == me + own, tail, 0.0), axis=1, keepdims=True)
+        slot = (lax.broadcasted_iota(jnp.int32, (chunk_toks, 1), 0) // rows * cap).astype(F32)
+        where_to = jnp.where(rank1 > 0.5, slot + rank1 - 1.0, -1.0)
+        column = lax.broadcasted_iota(jnp.int32, (chunk_toks, chunk_rows), 1).astype(F32)
+        select = (where_to == column).astype(BF16)
+        step = 512
+        select_t = select.T
+        for n in range(0, padded, step):
+            size = min(step, padded - n)
+            part = block[:, :, n:n + size].reshape(chunk_toks, size)
+            picked[:, n:n + size] = jnp.dot(select_t, part, preferred_element_type=F32).astype(BF16)
+        row_tail = picked[:, edge:].astype(F32)
+        row_lane = lax.broadcasted_iota(jnp.int32, (chunk_rows, 128), 1)
+        scale = jnp.sum(jnp.where(row_lane == me + (own + experts), row_tail, 0.0), axis=1, keepdims=True) * (1.0 / 32.0)
+
+        def ffn(cols):
+            x = picked[:, :width]
+            gate = jnp.dot(x, gate_w[:, cols], preferred_element_type=F32)
+            up = jnp.dot(x, up_w[:, cols], preferred_element_type=F32)
+            hid[:, cols] = (gate * jax.nn.sigmoid(1.702 * gate) * (up + 1.0)).astype(BF16)
+
+        whole, rest = tiles_of(half, 256)
+
+        def ffn_step(n, _):
+            ffn(pl.ds(pl.multiple_of(n * 256, 256), 256))
+            return 0
+
+        lax.fori_loop(0, whole, ffn_step, 0)
+        if rest:
+            ffn(pl.ds(whole * 256, rest))
+
+        def down(cols, size):
+            res = jnp.dot(hid[...], down_w[:, cols], preferred_element_type=F32) * scale
+            spread = jnp.dot(select, res.astype(BF16), preferred_element_type=F32).astype(BF16)
+            contrib[pl.ds(c * span, span), :, cols] = spread.reshape(span, rows, size)
+
+        whole2, rest2 = tiles_of(width, 512)
+
+        def down_step(n, _):
+            down(pl.ds(pl.multiple_of(n * 512, 512), 512), 512)
+            return 0
+
+        lax.fori_loop(0, whole2, down_step, 0)
+        if rest2:
+            down(pl.ds(whole2 * 512, rest2), rest2)
+
+    def stage(i, _):
+        c = 2 * i - i // 2 - 4 * (i // 3)
+
+        @pl.when((i == 1) | (i == 2))
+        def _():
+            def one(q, _):
+                k = c * groups + q
+                arrived(place(k))
+                to_core(k).start()
+                return 0
+
+            lax.fori_loop(0, groups, one, 0)
+
+        def got(q, _):
+            arrived(c * span + groups + q)
+            return 0
+
+        lax.fori_loop(0, groups, got, 0)
+
+        @pl.when(i == 3)
+        def _():
+            back_to_b(3)
+
+        chunk(c)
+        pair_copy(c).start()
+
+        @pl.when(i == 2)
+        def _():
+            back_to_b(2)
+
+        return 0
+
+    lax.fori_loop(0, 4, stage, 0)
+
+    pair_copy(1).wait_recv()
+
+    def a_step(j, _):
+        b_copy(groups + j).wait_recv()
+        s = place(groups + j)
+        contrib[s] = (contrib[s].astype(F32) + from_core[groups + j].astype(F32)
+                      + from_b[groups + j].astype(F32)).astype(BF16)
+        a_copy(j).start()
+        return 0
+
+    lax.fori_loop(0, groups, a_step, 0)
+    pair_copy(0).wait_recv()
+
+    for j in list(range(1, groups)) + [0]:
+        b_copy(j).wait_recv()
+        a_copy(j).wait_recv()
+        total = (contrib[j].astype(F32) + from_core[j].astype(F32)
+                 + from_b[j].astype(F32) + from_a[j].astype(F32))
+        if j:
+            contrib[j] = total.astype(BF16)
+            z_copy(j).start()
+        else:
+            for q in range(1, groups):
+                z_copy(groups - q).wait_recv()
+            for q in range(1, groups):
+                total = total + from_z[q].astype(F32)
+            out[...] = total.astype(BF16)
+
+    for j in range(1, groups):
+        to_z(j).wait_send()
+        z_copy(j).wait_send()
+    for j in range(groups):
+        to_a(j).wait_send()
+        a_copy(j).wait_send()
+    for c in range(4):
+        pair_copy(c).wait_send()
+    for k in range(2 * groups):
+        to_b(k).wait_send()
+        b_copy(k).wait_send()
+    for k in range(4 * groups):
+        to_core(k).wait_send()
+
+
+def gathered_plan(tokens, expert_ids, combine_int, gate_weight, up_weight, down_weight):
+    experts = lax.axis_size("expert")
+    rows, width = tokens.shape
+    cap = 2 * expert_ids.shape[1] * rows // experts
+    half = gate_weight.shape[2]
+    groups = experts // 4
+    padded = -(-width // 128) * 128
+    span = 2 * groups
+    vmem = pl.BlockSpec(memory_space=pltpu.VMEM)
+    anywhere = pl.BlockSpec(memory_space=pl.ANY)
+    dma = pltpu.SemaphoreType.DMA
+    flops = 2 * 4 * span * cap * width * half * 3
+    return pl.pallas_call(
+        functools.partial(kernel, experts, cap),
+        out_shape=jax.ShapeDtypeStruct((rows, width), BF16),
+        in_specs=[vmem] * 3 + [anywhere] * 3,
+        out_specs=vmem,
+        scratch_shapes=[
+            pltpu.VMEM((8 * groups, rows, padded), BF16),
+            pltpu.VMEM((8 * groups, rows, width), BF16),
+            pltpu.VMEM((4 * groups, rows, width), BF16),
+            pltpu.VMEM((2 * groups, rows, width), BF16),
+            pltpu.VMEM((groups, rows, width), BF16),
+            pltpu.VMEM((groups, rows, width), BF16),
+            pltpu.VMEM((span * cap, padded), BF16),
+            pltpu.VMEM((span * cap, half), BF16),
+            pltpu.VMEM((width, half), BF16),
+            pltpu.VMEM((width, half), BF16),
+            pltpu.VMEM((half, width), BF16),
+            dma((3,)),
+            dma((8 * groups,)),
+            dma((8 * groups,)),
+            dma((4,)),
+            dma((4,)),
+            dma((4 * groups,)),
+            dma((2 * groups,)),
+            dma((groups,)),
+            dma((groups,)),
+        ],
+        compiler_params=pltpu.CompilerParams(
+            collective_id=0, has_side_effects=True, vmem_limit_bytes=67043328),
+        cost_estimate=pl.CostEstimate(flops=flops, bytes_accessed=6 * width * half, transcendentals=0),
+    )(tokens, expert_ids, combine_int, gate_weight, up_weight, down_weight)
+
+
+def shards(tokens, expert_ids, *rest):
+    experts = lax.axis_size("expert")
+    rows, width = tokens.shape
+    cap = 2 * expert_ids.shape[1] * rows // experts
+    gathers = 2 * cap >= rows and experts % 4 == 0 and width % 128 + 2 * experts <= 128 and rows % 16 == 0 and width % 128 > 0
+    plan = gathered_plan if gathers else padded_plan
+    return plan(tokens, expert_ids, *rest)
 
 
 def solution(mesh):

time: 390 us -> 172 us (0.44)
  the two profiles are of different devices: /device:TPU:11 before, /device:TPU:2 now
where the time goes in v1:
time: 172 us; the launch traced here: 169 us
  Pallas kernels  141 us (82%)
  local copies, waits for them, and re-layouts  27.9 us (16%)
    pallas_call x1, Pallas kernels, gathered_plan(): pl.pallas_call(functools.partial(kernel, experts, cap), out_shape=jax.Sha...  141 us
    unnamed x5, local copies, waits for them, and re-layouts  27.9 us

profile of v1, /device:TPU:2, one launch (start us, length us, event | category | flops | bytes accessed | tf_op | source)
XLA Modules:
  0.0 169.4 jit_solution(2761223921105599531)
XLA Ops:
  0.0 1.4 copy.7.ids
  1.4 1.4 copy.8.comb
  2.7 11.7 %copy.9.gate_hbm = bf16[1,2880,1440]{2,1,0:T(8,128)(2,1)} copy(bf16[1,2880,1440]{1,2,0:T(8,128)(2,1)} %param.9) | data formatting | bytes 16588800 | tf_op args[3]
  14.5 11.8 %copy.10.up_hbm = bf16[1,2880,1440]{2,1,0:T(8,128)(2,1)} copy(bf16[1,2880,1440]{1,2,0:T(8,128)(2,1)} %param.10) | data formatting | bytes 16588800 | tf_op args[4]
  26.2 141.4 %shard_map.64 = bf16[48,2880]{1,0:T(8,128)(2,1)} custom-call(bf16[48,2880]{1,0:T(8,128)(2,1)} %tokens.1, s32[48,4]{1,0:T(8,128)} %copy.7.ids, s32[48,4]{1,0:T(8,128)} %copy.8.comb, bf16[1,2880,1440]{2,1,0:T(8,128)(2,1)} %copy.9.gate_hbm, bf16[1,2880,1440]{2,1,0:T(8,128)(2,1)} %copy.10.up_hbm, bf16[1,1440,2880]{2,1,0:T(8,128)(2,1)} %down_hbm.1), custom_call_target="tpu_custom_call" | custom-call | flops 19110297600 | bytes 24883200 | tf_op jit(solution)/shard_map/pallas_call | solution.py:318
  167.7 1.7 copy.12

commit v2 on v1

--- a/solution.py
+++ b/solution.py
@@ -10,6 +10,7 @@
 MESH = pl.DeviceIdType.MESH
 BF16 = jnp.bfloat16
 F32 = jnp.float32
+LAST = (((1,), (1,)), ((), ()))
 
 
 def expert_rows(rows, gate_w, up_w, down_w):
@@ -54,13 +55,15 @@
     return total // step, total % step
 
 
-def kernel(experts, cap, tokens, ids, comb, gate_hbm, up_hbm, down_hbm, out,
-           tok, contrib, from_core, from_b, from_a, from_z, picked, hid, gate_w, up_w, down_w,
-           w_sem, send_sem, recv_sem, pair_send, pair_recv, ret_send, b_recv, a_recv, z_recv):
+def kernel(experts, cap, tokens, ids_t, comb_t, gate_hbm, up_hbm, down_hbm, out,
+           tok, contrib, from_core, from_b, from_a, from_z, acc, picked, hid, gate_w, up_w, down_w,
+           w_sem, send_sem, recv_sem, pair_send, pair_recv, ret_send, b_recv, a_recv,
+           z_send, zr_send, z_recv):
     rows, width = tokens.shape
-    half = gate_w.shape[1]
+    half = gate_w.shape[0]
     padded = tok.shape[2]
-    top = ids.shape[1]
+    top = ids_t.shape[0]
+    ids, comb = ids_t[...].T, comb_t[...].T
     groups = experts // 4
     span = 2 * groups
     me, dp = lax.axis_index("expert"), lax.axis_index("dp")
@@ -69,14 +72,30 @@
     a_peer = (me + (1 - core) * (2 - 4 * side), dp + core * (1 - 2 * dp))
     b_peer = (me + core * (2 - 4 * side), dp + (1 - core) * (1 - 2 * dp))
 
-    def z_peer(j):
-        return (((g + j) % groups) * 4 + me % 4, dp)
+    def z_peer(way):
+        return (me + 4 * way, dp)
+
+    def follows(way):
+        return g < groups - 1 if way > 0 else g > 0
+
+    def inside(z):
+        return (z >= 0) & (z < groups)
 
     loads = [
         pltpu.make_async_copy(gate_hbm.at[0], gate_w, w_sem.at[0]),
         pltpu.make_async_copy(up_hbm.at[0], up_w, w_sem.at[1]),
         pltpu.make_async_copy(down_hbm.at[0], down_w, w_sem.at[2]),
     ]
+
+    for load in loads:
+        load.start()
+    barrier = pltpu.get_barrier_semaphore()
+    for peer in (partner, a_peer, b_peer):
+        pl.semaphore_signal(barrier, inc=1, device_id=peer, device_id_type=MESH)
+    for way in (1, -1):
+        @pl.when(follows(way))
+        def _():
+            pl.semaphore_signal(barrier, inc=1, device_id=z_peer(way), device_id_type=MESH)
 
     edge = padded - 128
     own = width - edge
@@ -90,14 +109,11 @@
              >= lax.broadcasted_iota(jnp.int32, (rows, rows), 1)).astype(BF16)
     counts = jnp.dot(below, hits.astype(BF16), preferred_element_type=F32)
     info = (hits * counts + weights).astype(BF16)
-    tok[0, :, :edge] = tokens[:, :edge]
-    tok[0, :, edge:] = jnp.concatenate([tokens[:, edge:width], info[:, own:]], axis=1)
-
-    barrier = pltpu.get_barrier_semaphore()
-    peers = [partner, a_peer, b_peer] + [z_peer(j) for j in range(1, groups)]
-    for peer in peers:
-        pl.semaphore_signal(barrier, inc=1, device_id=peer, device_id_type=MESH)
-    pl.semaphore_wait(barrier, len(peers))
+    tok[g, :, :edge] = tokens[:, :edge]
+    tok[g, :, edge:] = jnp.concatenate([tokens[:, edge:width], info[:, own:]], axis=1)
+
+    neighbours = (g + groups - 1) // groups + (2 * groups - 2 - g) // groups
+    pl.semaphore_wait(barrier, 3 + neighbours)
 
     def place(k):
         return (k // groups) * span + k % groups
@@ -107,8 +123,10 @@
             src_ref=tok.at[src], dst_ref=tok.at[dst], send_sem=send_sem.at[sem],
             recv_sem=recv_sem.at[dst], device_id=peer, device_id_type=MESH)
 
-    def to_z(j):
-        return sent(0, groups - j, j, z_peer(j))
+    def to_z(src, way):
+        return pltpu.make_async_remote_copy(
+            src_ref=tok.at[src], dst_ref=tok.at[src], send_sem=z_send.at[(1 - way) // 2, src],
+            recv_sem=recv_sem.at[src], device_id=z_peer(way), device_id_type=MESH)
 
     def to_a(j):
         return sent(place(j), place(groups + j), groups + j, a_peer)
@@ -122,22 +140,41 @@
     def arrived(slot):
         sent(0, slot, 0, partner).wait_recv()
 
-    for j in range(1, groups):
-        to_z(j).start()
-    to_a(0).start()
-    to_b(0).start()
-    to_core(0).start()
-    for load in loads:
-        load.start()
-    for j in range(1, groups):
-        arrived(place(j))
-        to_a(j).start()
-        to_b(j).start()
-        to_core(j).start()
-    for j in range(groups):
-        arrived(place(groups + j))
-        to_b(groups + j).start()
-        to_core(groups + j).start()
+    def spread_out(k):
+        to_a(k).start()
+        to_b(k).start()
+        to_core(k).start()
+
+    def pass_on(z):
+        arrived(place(groups + z))
+        to_b(groups + z).start()
+        to_core(groups + z).start()
+
+    for way in (1, -1):
+        @pl.when(follows(way))
+        def _():
+            to_z(g, way).start()
+    spread_out(g)
+    for d in range(1, groups + 1):
+        if d < groups:
+            for way in (1, -1):
+                src = g - way * d
+
+                @pl.when(inside(src))
+                def _():
+                    arrived(src)
+
+                    @pl.when(follows(way))
+                    def _():
+                        to_z(src, way).start()
+
+                    spread_out(src)
+        for way in (1, -1) if d > 1 else (1,):
+            src = g - way * (d - 1)
+
+            @pl.when(inside(src))
+            def _():
+                pass_on(src)
     for load in loads:
         load.wait()
 
@@ -156,16 +193,22 @@
             src_ref=contrib.at[place(groups + j)], dst_ref=from_a.at[j],
             send_sem=ret_send.at[groups + j], recv_sem=a_recv.at[j], device_id=a_peer, device_id_type=MESH)
 
-    def z_copy(j):
-        return pltpu.make_async_remote_copy(
-            src_ref=contrib.at[j], dst_ref=from_z.at[groups - j],
-            send_sem=ret_send.at[j], recv_sem=z_recv.at[groups - j], device_id=z_peer(j), device_id_type=MESH)
+    def z_copy(z, way):
+        return pltpu.make_async_remote_copy(
+            src_ref=contrib.at[z], dst_ref=from_z.at[(1 - way) // 2, z],
+            send_sem=zr_send.at[(1 - way) // 2, z], recv_sem=z_recv.at[(1 - way) // 2, z],
+            device_id=z_peer(way), device_id_type=MESH)
+
+    upper = g // (groups // 2)
+
+    def far_first(t):
+        return t * upper + (groups - 1 - t) * (1 - upper)
 
     def back_to_b(c):
         pair_copy(c).wait_recv()
 
         def one(q, _):
-            k = c * groups + q
+            k = c * groups + far_first(q)
             s = place(k)
             contrib[s] = (contrib[s].astype(F32) + from_core[k].astype(F32)).astype(BF16)
             b_copy(k - 2 * groups).start()
@@ -197,8 +240,8 @@
 
         def ffn(cols):
             x = picked[:, :width]
-            gate = jnp.dot(x, gate_w[:, cols], preferred_element_type=F32)
-            up = jnp.dot(x, up_w[:, cols], preferred_element_type=F32)
+            gate = lax.dot_general(x, gate_w[cols, :], LAST, preferred_element_type=F32)
+            up = lax.dot_general(x, up_w[cols, :], LAST, preferred_element_type=F32)
             hid[:, cols] = (gate * jax.nn.sigmoid(1.702 * gate) * (up + 1.0)).astype(BF16)
 
         whole, rest = tiles_of(half, 256)
@@ -227,17 +270,17 @@
             down(pl.ds(whole2 * 512, rest2), rest2)
 
     def stage(i, _):
-        c = 2 * i - i // 2 - 4 * (i // 3)
-
-        @pl.when((i == 1) | (i == 2))
+        c = (4 - i) % 4
+
+        @pl.when(i == 1)
         def _():
             def one(q, _):
-                k = c * groups + q
+                k = 2 * groups + q
                 arrived(place(k))
                 to_core(k).start()
                 return 0
 
-            lax.fori_loop(0, groups, one, 0)
+            lax.fori_loop(0, 2 * groups, one, 0)
 
         def got(q, _):
             arrived(c * span + groups + q)
@@ -247,14 +290,14 @@
 
         @pl.when(i == 3)
         def _():
-            back_to_b(3)
+            back_to_b(2)
 
         chunk(c)
         pair_copy(c).start()
 
         @pl.when(i == 2)
         def _():
-            back_to_b(2)
+            back_to_b(3)
 
         return 0
 
@@ -262,7 +305,8 @@
 
     pair_copy(1).wait_recv()
 
-    def a_step(j, _):
+    def a_step(t, _):
+        j = far_first(t)
         b_copy(groups + j).wait_recv()
         s = place(groups + j)
         contrib[s] = (contrib[s].astype(F32) + from_core[groups + j].astype(F32)
@@ -273,27 +317,48 @@
     lax.fori_loop(0, groups, a_step, 0)
     pair_copy(0).wait_recv()
 
-    for j in list(range(1, groups)) + [0]:
-        b_copy(j).wait_recv()
-        a_copy(j).wait_recv()
-        total = (contrib[j].astype(F32) + from_core[j].astype(F32)
-                 + from_b[j].astype(F32) + from_a[j].astype(F32))
-        if j:
-            contrib[j] = total.astype(BF16)
-            z_copy(j).start()
-        else:
-            for q in range(1, groups):
-                z_copy(groups - q).wait_recv()
-            for q in range(1, groups):
-                total = total + from_z[q].astype(F32)
-            out[...] = total.astype(BF16)
-
-    for j in range(1, groups):
-        to_z(j).wait_send()
-        z_copy(j).wait_send()
-    for j in range(groups):
-        to_a(j).wait_send()
-        a_copy(j).wait_send()
+    def gathered(z):
+        return (contrib[z].astype(F32) + from_core[z].astype(F32)
+                + from_b[z].astype(F32) + from_a[z].astype(F32))
+
+    def z_step(t, _):
+        z = far_first(t)
+        b_copy(z).wait_recv()
+        a_copy(z).wait_recv()
+        acc[...] = gathered(z)
+        for way in (1, -1):
+            @pl.when((z - g) * way > 0)
+            def _():
+                @pl.when(follows(-way))
+                def _():
+                    z_copy(z, way).wait_recv()
+                    acc[...] += from_z[(1 - way) // 2, z].astype(F32)
+
+                contrib[z] = acc[...].astype(BF16)
+                z_copy(z, way).start()
+
+        return 0
+
+    lax.fori_loop(0, groups, z_step, 0)
+    acc[...] = gathered(g)
+    for way in (1, -1):
+        @pl.when(follows(-way))
+        def _():
+            z_copy(g, way).wait_recv()
+            acc[...] += from_z[(1 - way) // 2, g].astype(F32)
+    out[...] = acc[...].astype(BF16)
+
+    for z in range(groups):
+        for way in (1, -1):
+            @pl.when(follows(way) & ((g - z) * way >= 0))
+            def _():
+                to_z(z, way).wait_send()
+
+            @pl.when((z - g) * way > 0)
+            def _():
+                z_copy(z, way).wait_send()
+        to_a(z).wait_send()
+        a_copy(z).wait_send()
     for c in range(4):
         pair_copy(c).wait_send()
     for k in range(2 * groups):
@@ -326,11 +391,12 @@
             pltpu.VMEM((4 * groups, rows, width), BF16),
             pltpu.VMEM((2 * groups, rows, width), BF16),
             pltpu.VMEM((groups, rows, width), BF16),
-            pltpu.VMEM((groups, rows, width), BF16),
+            pltpu.VMEM((2, groups, rows, width), BF16),
+            pltpu.VMEM((rows, width), F32),
             pltpu.VMEM((span * cap, padded), BF16),
             pltpu.VMEM((span * cap, half), BF16),
-            pltpu.VMEM((width, half), BF16),
-            pltpu.VMEM((width, half), BF16),
+            pltpu.VMEM((half, width), BF16),
+            pltpu.VMEM((half, width), BF16),
             pltpu.VMEM((half, width), BF16),
             dma((3,)),
             dma((8 * groups,)),
@@ -340,12 +406,14 @@
             dma((4 * groups,)),
             dma((2 * groups,)),
             dma((groups,)),
-            dma((groups,)),
+            dma((2, groups)),
+            dma((2, groups)),
+            dma((2, groups)),
         ],
         compiler_params=pltpu.CompilerParams(
             collective_id=0, has_side_effects=True, vmem_limit_bytes=67043328),
         cost_estimate=pl.CostEstimate(flops=flops, bytes_accessed=6 * width * half, transcendentals=0),
-    )(tokens, expert_ids, combine_int, gate_weight, up_weight, down_weight)
+    )(tokens, expert_ids.T, combine_int.T, jnp.swapaxes(gate_weight, 1, 2), jnp.swapaxes(up_weight, 1, 2), down_weight)
 
 
 def shards(tokens, expert_ids, *rest):

time: 172 us -> 128 us (0.74)
  local copies, waits for them, and re-layouts: 27.9 us -> 1.69 us
  Pallas kernels: 141 us -> 124 us
    unnamed x5 -> x1, local copies, waits for them, and re-layouts: 27.9 us -> 1.69 us
    pallas_call x1, Pallas kernels: 141 us -> 124 us  [gathered_plan(): pl.pallas_call(functools.partial(kernel, experts, cap), out_shape=jax.Sha...]
where the time goes in v2:
time: 128 us; the launch traced here: 126 us
  Pallas kernels  124 us (97%)
  local copies, waits for them, and re-layouts  1.69 us (1%)
    pallas_call x1, Pallas kernels, gathered_plan(): pl.pallas_call(functools.partial(kernel, experts, cap), out_shape=jax.Sha...  124 us

profile of v2, /device:TPU:2, one launch (start us, length us, event | category | flops | bytes accessed | tf_op | source)
XLA Modules:
  0.0 125.7 jit_solution(54961685217684486)
XLA Ops:
  0.0 124.0 %shard_map.64 = bf16[48,2880]{1,0:T(8,128)(2,1)} custom-call(bf16[48,2880]{1,0:T(8,128)(2,1)} %tokens.1, s32[4,48]{1,0:T(4,128)} %bitcast.6, s32[4,48]{1,0:T(4,128)} %bitcast.7, bf16[1,1440,2880]{2,1,0:T(8,128)(2,1)} %bitcast.4, bf16[1,1440,2880]{2,1,0:T(8,128)(2,1)} %bitcast.5, bf16[1,1440,2880]{2,1,0:T(8,128)(2,1)} %down_hbm.1), custom_call_target="tpu_custom_call" | custom-call | flops 19110297600 | bytes 24883200 | tf_op jit(solution)/shard_map/pallas_call | solution.py:383
  124.0 1.7 %copy.8 = bf16[48,2880]{1,0:T(8,128)(2,1)} copy(bf16[48,2880]{1,0:T(8,128)(2,1)} %shard_map.64) | data formatting | bytes 552960

commit v3 on v2

--- a/solution.py
+++ b/solution.py
@@ -11,6 +11,9 @@
 BF16 = jnp.bfloat16
 F32 = jnp.float32
 LAST = (((1,), (1,)), ((), ()))
+PAUSE = 0
+FTILE = 768
+DTILE = 1408
 
 
 def expert_rows(rows, gate_w, up_w, down_w):
@@ -219,7 +222,7 @@
     chunk_rows = span * cap
     chunk_toks = span * rows
 
-    def chunk(c):
+    def chunk(c, meanwhile):
         block = tok.at[pl.ds(c * span, span)]
         tail = block[:, :, edge:].reshape(chunk_toks, 128).astype(F32)
         tail_lane = lax.broadcasted_iota(jnp.int32, (chunk_toks, 128), 1)
@@ -244,30 +247,31 @@
             up = lax.dot_general(x, up_w[cols, :], LAST, preferred_element_type=F32)
             hid[:, cols] = (gate * jax.nn.sigmoid(1.702 * gate) * (up + 1.0)).astype(BF16)
 
-        whole, rest = tiles_of(half, 256)
+        whole, rest = tiles_of(half, FTILE)
 
         def ffn_step(n, _):
-            ffn(pl.ds(pl.multiple_of(n * 256, 256), 256))
+            meanwhile(n)
+            ffn(pl.ds(pl.multiple_of(n * FTILE, FTILE), FTILE))
             return 0
 
         lax.fori_loop(0, whole, ffn_step, 0)
         if rest:
-            ffn(pl.ds(whole * 256, rest))
+            ffn(pl.ds(whole * FTILE, rest))
 
         def down(cols, size):
             res = jnp.dot(hid[...], down_w[:, cols], preferred_element_type=F32) * scale
             spread = jnp.dot(select, res.astype(BF16), preferred_element_type=F32).astype(BF16)
             contrib[pl.ds(c * span, span), :, cols] = spread.reshape(span, rows, size)
 
-        whole2, rest2 = tiles_of(width, 512)
+        whole2, rest2 = tiles_of(width, DTILE)
 
         def down_step(n, _):
-            down(pl.ds(pl.multiple_of(n * 512, 512), 512), 512)
+            down(pl.ds(pl.multiple_of(n * DTILE, DTILE), DTILE), DTILE)
             return 0
 
         lax.fori_loop(0, whole2, down_step, 0)
         if rest2:
-            down(pl.ds(whole2 * 512, rest2), rest2)
+            down(pl.ds(whole2 * DTILE, rest2), rest2)
 
     def stage(i, _):
         c = (4 - i) % 4
@@ -288,17 +292,13 @@
 
         lax.fori_loop(0, groups, got, 0)
 
-        @pl.when(i == 3)
-        def _():
-            back_to_b(2)
-
-        chunk(c)
+        def meanwhile(n):
+            @pl.when((n == PAUSE) & (i >= 2))
+            def _():
+                back_to_b((c + 1) % 4)
+
+        chunk(c, meanwhile)
         pair_copy(c).start()
-
-        @pl.when(i == 2)
-        def _():
-            back_to_b(3)
-
         return 0
 
     lax.fori_loop(0, 4, stage, 0)

time: 128 us -> 119 us (0.930); the launches traced: 126 us -> 119 us
  Pallas kernels: 124 us -> 117 us
    pallas_call x1, Pallas kernels: 124 us -> 117 us  [gathered_plan(): pl.pallas_call(functools.partial(kernel, experts, cap), out_shape=jax.Sha...]
where the time goes in v3:
time: 119 us
  Pallas kernels  117 us (98%)
  local copies, waits for them, and re-layouts  1.69 us (1%)
    pallas_call x1, Pallas kernels, gathered_plan(): pl.pallas_call(functools.partial(kernel, experts, cap), out_shape=jax.Sha...  117 us

profile of v3, /device:TPU:2, one launch (start us, length us, event | category | flops | bytes accessed | tf_op | source)
XLA Modules:
  0.0 118.5 jit_solution(10560096377832814103)
XLA Ops:
  0.0 116.8 %shard_map.64 = bf16[48,2880]{1,0:T(8,128)(2,1)} custom-call(bf16[48,2880]{1,0:T(8,128)(2,1)} %tokens.1, s32[4,48]{1,0:T(4,128)} %bitcast.6, s32[4,48]{1,0:T(4,128)} %bitcast.7, bf16[1,1440,2880]{2,1,0:T(8,128)(2,1)} %bitcast.4, bf16[1,1440,2880]{2,1,0:T(8,128)(2,1)} %bitcast.5, bf16[1,1440,2880]{2,1,0:T(8,128)(2,1)} %down_hbm.1), custom_call_target="tpu_custom_call" | custom-call | flops 19110297600 | bytes 24883200 | tf_op jit(solution)/shard_map/pallas_call | solution.py:383
  116.8 1.7 %copy.8 = bf16[48,2880]{1,0:T(8,128)(2,1)} copy(bf16[48,2880]{1,0:T(8,128)(2,1)} %shard_map.64) | data formatting | bytes 552960

commit v4 on v3

--- a/solution.py
+++ b/solution.py
@@ -13,7 +13,7 @@
 LAST = (((1,), (1,)), ((), ()))
 PAUSE = 0
 FTILE = 768
-DTILE = 1408
+DTILE = 1536
 
 
 def expert_rows(rows, gate_w, up_w, down_w):

time: 119 us -> 116 us (0.975)
  Pallas kernels: 117 us -> 113 us
    pallas_call x1, Pallas kernels: 117 us -> 113 us  [gathered_plan(): pl.pallas_call(functools.partial(kernel, experts, cap), out_shape=jax.Sha...]
where the time goes in v4:
time: 116 us; the launch traced here: 115 us
  Pallas kernels  113 us (97%)
  local copies, waits for them, and re-layouts  1.69 us (1%)
    pallas_call x1, Pallas kernels, gathered_plan(): pl.pallas_call(functools.partial(kernel, experts, cap), out_shape=jax.Sha...  113 us

profile of v4, /device:TPU:2, one launch (start us, length us, event | category | flops | bytes accessed | tf_op | source)
XLA Modules:
  0.0 114.6 jit_solution(7503764008410054954)
XLA Ops:
  0.0 112.9 %shard_map.64 = bf16[48,2880]{1,0:T(8,128)(2,1)} custom-call(bf16[48,2880]{1,0:T(8,128)(2,1)} %tokens.1, s32[4,48]{1,0:T(4,128)} %bitcast.6, s32[4,48]{1,0:T(4,128)} %bitcast.7, bf16[1,1440,2880]{2,1,0:T(8,128)(2,1)} %bitcast.4, bf16[1,1440,2880]{2,1,0:T(8,128)(2,1)} %bitcast.5, bf16[1,1440,2880]{2,1,0:T(8,128)(2,1)} %down_hbm.1), custom_call_target="tpu_custom_call" | custom-call | flops 19110297600 | bytes 24883200 | tf_op jit(solution)/shard_map/pallas_call | solution.py:383
  112.9 1.7 %copy.8 = bf16[48,2880]{1,0:T(8,128)(2,1)} copy(bf16[48,2880]{1,0:T(8,128)(2,1)} %shard_map.64) | data formatting | bytes 552960
